TPU v7x, 256 devices: a whole 4x4x8 slice. The times are simulated.
256 devices in a mesh: ctx: 8 (over x, y_hi), chan: 32 (over z, y_lo, core).
Axes of the slice: x: 4, y: 4 (y_hi: 2, y_lo: 2; y = y_hi * 2 + y_lo), z: 8, core: 2. Of those that a mesh axis runs over, the one named last changes fastest.
Arguments:
- inputs: bfloat16 [4096, 4096], P('ctx', 'chan'), may hold values from -6 to 6
- w_in: bfloat16 [4096, 3, 4096], P(None, None, 'chan'), may hold values from -0.09375 to 0.09375
- conv_taps: bfloat16 [3, 3, 4096], P(None, None, 'chan'), may hold values from -3.59375 to 3.59375
- skip_gain: float32 [4096], P('chan'), may hold values from 0.5 to 1.5
- filter_taps: bfloat16 [4096, 4096], P('ctx', 'chan'), may hold values from -0.09375 to 0.09375
- w_out: bfloat16 [4096, 4096], P('chan'), may hold values from -0.1875 to 0.1875
Outputs:
- result: bfloat16 [4096, 4096], P('ctx', 'chan')
All inputs are finite; a program needn't handle non-finite values.
Results may differ from a plain program's by a relative error of at most 0.024.
Values may be sent and summed in bfloat16 or wider, within the bound.
A program may use at most 64 MiB of HBM per device.

v0:
```python
import math
import jax
import jax.numpy as jnp
from jax import lax
from jax.sharding import PartitionSpec as P

KERNEL = 3


def from_behind(block, axis, distance):
    devices = range(lax.axis_size(axis))
    route = [(i - distance, i) for i in devices if i - distance in devices]
    return lax.ppermute(block, axis, route)


def angles(row_count, col_count, double_len):
    row_ids = jnp.arange(row_count, dtype=jnp.int32)[:, None]
    col_ids = jnp.arange(col_count, dtype=jnp.int32)[None, :]
    return 2.0 * math.pi / double_len * (row_ids * col_ids % double_len).astype(jnp.float32)


def tables(span_len):
    double_len = 2 * span_len
    first = angles(double_len, span_len, double_len)
    forward_in = jnp.concatenate([jnp.cos(first), -jnp.sin(first)], 0).astype(jnp.bfloat16)
    second = angles(double_len, double_len, double_len)
    forward_taps = jnp.concatenate([jnp.cos(second), -jnp.sin(second)], 0).astype(jnp.bfloat16)
    third = angles(span_len, double_len, double_len)
    inverse = (jnp.concatenate([jnp.cos(third), -jnp.sin(third)], 1) / double_len).astype(
        jnp.bfloat16
    )
    return (forward_in, forward_taps, inverse)


def body(inputs, w_in, conv_taps, skip_gain, filter_taps, w_out):
    span_len, width_dev = inputs.shape
    double_len = 2 * span_len
    groups = lax.axis_size("ctx")
    position = lax.axis_index("ctx")
    w_flat = w_in.reshape(w_in.shape[0], 3 * width_dev)
    projected = jnp.dot(
        lax.all_gather(inputs, "chan", axis=1, tiled=True),
        w_flat,
        preferred_element_type=jnp.float32,
    )
    by_stream = projected.astype(jnp.bfloat16).reshape(span_len, 3, width_dev)
    rim_rows = from_behind(by_stream[span_len - (KERNEL - 1) :], "ctx", 1)
    padded = jnp.concatenate([rim_rows, by_stream], 0)
    filtered = jnp.zeros((span_len, 3, width_dev), jnp.float32)
    for lag in range(KERNEL):
        start_row = KERNEL - 1 - lag
        filtered = filtered + conv_taps[lag].astype(jnp.float32) * padded[
            start_row : start_row + span_len
        ].astype(jnp.float32)
    streams = filtered.astype(jnp.bfloat16)
    gate_out = streams[:, 0]
    gated_in = (streams[:, 1].astype(jnp.float32) * streams[:, 2].astype(jnp.float32)).astype(
        jnp.bfloat16
    )
    forward_in, forward_taps, inverse = tables(span_len)
    all_taps = lax.all_gather(filter_taps[None], "ctx", axis=0, tiled=True)
    previous = jnp.concatenate(
        [jnp.zeros((1, span_len, width_dev), jnp.bfloat16), all_taps[:-1]], 0
    )
    padded_taps = jnp.concatenate(
        [all_taps, jnp.zeros((groups, 1, width_dev), jnp.bfloat16), previous[:, 1:]], 1
    )
    spectra_taps = jnp.einsum(
        "fm,kmd->kfd", forward_taps, padded_taps, preferred_element_type=jnp.float32
    ).astype(jnp.bfloat16)

    def accumulate(spectra):
        pieces = spectra.shape[0]
        lag_index = position - jnp.arange(pieces, dtype=jnp.int32)
        causal = lag_index >= 0
        chosen = jnp.take(spectra_taps, jnp.clip(lag_index, 0, groups - 1), axis=0)
        real_g = chosen[:, :double_len].astype(jnp.float32)
        imag_g = chosen[:, double_len:].astype(jnp.float32)
        real_u = spectra[:, :double_len].astype(jnp.float32)
        imag_u = spectra[:, double_len:].astype(jnp.float32)
        product = jnp.concatenate(
            [real_g * real_u - imag_g * imag_u, real_g * imag_u + imag_g * real_u], 1
        )
        product = jnp.where(causal[:, None, None], product, 0.0)
        return jnp.sum(product, axis=0)

    empty = jnp.zeros((2 * double_len, width_dev), jnp.float32)
    incoming = lax.all_gather(gated_in[None], "ctx", axis=0, tiled=True)

    def transform(current):
        spectra = jnp.einsum(
            "fb,mbc->mfc", forward_in, incoming, preferred_element_type=jnp.float32
        ).astype(jnp.bfloat16)
        return accumulate(spectra)

    def unchanged(current):
        return current

    mixture = lax.cond(jnp.int32(0) <= position, transform, unchanged, empty)
    long_out = jnp.dot(inverse, mixture.astype(jnp.bfloat16), preferred_element_type=jnp.float32)
    long_out = long_out + skip_gain * gated_in.astype(jnp.float32)
    gated_out = (gate_out.astype(jnp.float32) * long_out).astype(jnp.bfloat16)
    shares = lax.psum_scatter(
        lax.dot_general(
            w_out, gated_out, (((0,), (1,)), ((), ())), preferred_element_type=jnp.float32
        ).astype(jnp.bfloat16),
        "chan",
        scatter_dimension=0,
        tiled=True,
    ).astype(jnp.float32)
    result = shares.T.astype(jnp.bfloat16)
    return result


def solution(mesh):
    return jax.shard_map(
        body,
        mesh=mesh,
        in_specs=(
            P("ctx", "chan"),
            P(None, None, "chan"),
            P(None, None, "chan"),
            P("chan"),
            P("ctx", "chan"),
            P("chan", None),
        ),
        out_specs=P("ctx", "chan"),
        check_vma=False,
    )
```

profile of v0, /device:TPU:2, one launch (start us, length us, event | category | flops | bytes accessed | tf_op | source)
XLA Modules:
  0.0 362.8 jit_solution(12032733363743126009)
XLA Ops:
  6.5 0.0 copy-start
  6.5 0.0 all-gather.6.cloned.1.call-start
  6.5 0.7 all-gather.6.cloned.1.call-update
  7.3 0.0 all-gather.8.cloned.1.call-start
  7.3 0.7 all-gather.8.cloned.1.call-update
  8.0 0.0 all-gather.10.cloned.1.call-start
  8.1 4.8 %copy.23 = bf16[4096,3,128]{0,2,1:T(8,128)(2,1)} copy(bf16[4096,3,128]{2,0,1:T(8,128)(2,1)} %param.9) | data formatting | bytes 6291456 | tf_op args[1]
  12.8 9.3 %negate_convert_fusion.1 = (bf16[1024,512]{1,0:T(8,128)(2,1)}, bf16[1024,512]{1,0:T(8,128)(2,1)}) fusion(), kind=kLoop, calls=%fused_computation.56 | loop fusion | flops 8912896 | bytes 2097152 | tf_op jit(solution)/shard_map/convert.8
  22.1 62.3 %all-gather.6.cloned.1.call-done = bf16[512,4096]{1,0:T(8,128)(2,1)} async-done(((bf16[512,128]{1,0:T(8,128)(2,1)}), bf16[512,4096]{1,0:T(8,128)(2,1)}) %all-gather.6.cloned.1.call-update) | async-done | bytes 4194320 | tf_op jit(solution)/shard_map/all_gather | solution.py:42
  84.4 0.0 copy-start.2
  84.4 5.5 %convolution_convert_fusion.1 = bf16[512,384]{1,0:T(8,128)(2,1)S(1)} fusion(bf16[512,4096]{1,0:T(8,128)(2,1)} %all-gather.6.cloned.1.call-done, bf16[4096,384]{0,1:T(8,128)(2,1)} %bitcast.54), kind=kOutput, calls=%fused_computation.66 | convolution fusion | flops 1610809344 | bytes 7733248 | tf_op jit(solution)/shard_map/dot_general | solution.py:41
  89.9 4.9 %collective-permute-start = (bf16[2,3,128]{2,0,1:T(2,128)(2,1)S(1)}, bf16[2,3,128]{2,0,1:T(2,128)(2,1)S(1)}, u32[]{:S(2)}, u32[]{:S(2)}) collective-permute-start(bf16[2,3,128]{2,0,1:T(2,128)(2,1)S(1)} %slice_bitcast_fusion.2), channel_id=1, source_target_pairs={{0,32},{32,64},{64,96},{96,128},{128,160},{160,192},{192,224},{1,3... | collective-permute-start | bytes 4616 | tf_op jit(solution)/shard_map/ppermute | solution.py:13
  94.9 0.0 copy-done.2
  94.9 0.2 copy.24
  95.1 0.2 copy.25
  95.3 2.5 collective-permute-done
  97.8 0.3 add_convert_fusion
  98.1 0.7 multiply_convert_fusion
  98.8 0.0 all-gather.10.cloned.1.call-update
  98.8 0.2 reduce-scatter.4.cloned.1.call-start
  99.0 9.1 %sine_negate_fusion = (f32[512,1024]{1,0:T(8,128)S(1)}, f32[512,1024]{1,0:T(8,128)}) fusion(), kind=kLoop, calls=%fused_computation.60 | loop fusion | flops 7864320 | bytes 4194304 | tf_op jit(solution)/shard_map/neg | solution.py:29
  108.2 3.0 pad_maximum_fusion
  111.1 17.8 %negate_convert_fusion = (bf16[1024,1024]{1,0:T(8,128)(2,1)}, bf16[1024,1024]{1,0:T(8,128)(2,1)}) fusion(), kind=kLoop, calls=%fused_computation.34 | loop fusion | flops 17825792 | bytes 4194304 | tf_op jit(solution)/shard_map/convert.6
  129.0 8.9 %all-gather.8.cloned.1.call-done = bf16[4096,128]{1,0:T(8,128)(2,1)} async-done(((bf16[512,128]{1,0:T(8,128)(2,1)}), bf16[4096,128]{1,0:T(8,128)(2,1)}) %all-gather.8.cloned.1.call-update) | async-done | bytes 1048592 | tf_op jit(solution)/shard_map/all_gather | solution.py:61
  137.9 2.2 slice.71
  140.0 2.3 copy.28
  142.3 2.3 copy.29
  144.6 1.6 pad_slice_fusion
  146.2 9.1 %convert_bitcast_fusion.1 = bf16[8,2048,128]{1,2,0:T(8,128)(2,1)} fusion(bf16[1024,1024]{1,0:T(8,128)(2,1)} %get-tuple-element.40, bf16[1024,1024]{1,0:T(8,128)(2,1)} %get-tuple-element.41, bf16[8,511,128]{1,2,0:T(8,128)(2,1)S(1)} %pad_slice_fusion, bf16[8,512,128]{1,2,0:T(8,128)(2,1)} %copy.29, bf16[1024]{0:T(1024)(128)(2,1)S(1)} %pad.8.clone), kind=kOutput, calls=%fused_computation.33 | convolution fusion | flops 4311744512 | bytes 10485760 | tf_op jit(solution)/shard_map/fm,kmd->kfd/dot_general | solution.py:68
  155.2 36.6 %all-gather.10.cloned.1.call-done = bf16[4096,1,128]{2,0,1:T(8,128)(2,1)} async-done(((bf16[512,1,128]{2,0,1:T(8,128)(2,1)}), bf16[4096,1,128]{2,0,1:T(8,128)(2,1)}) %all-gather.10.cloned.1.call-update) | async-done | bytes 1048592 | tf_op jit(solution)/shard_map/all_gather | solution.py:88
  191.8 0.0 copy-start.3
  191.8 28.0 %conditional.1 = (bf16[2048,128]{0,1:T(8,128)(2,1)}) conditional(s32[]{:T(128)} %convert_element_type.147, () %tuple.13, (s32[]{:T(128)}, bf16[8,2048,128]{1,2,0:T(8,128)(2,1)}, bf16[8,512,128]{2,1,0:T(8,128)(2,1)}, bf16[2048,512]{1,0:T(8,128)(2,1)}) %tuple.35), branch_computations={%region_0.1_spmd, %region_1.3_spmd} | conditional | flops 2168194048 | bytes 79171784 | solution.py:99
  191.9 6.5 %copy.30 = bf16[8,2048,128]{2,1,0:T(8,128)(2,1)} copy(bf16[8,2048,128]{1,2,0:T(8,128)(2,1)} %get-tuple-element.30) | data formatting | bytes 8388608 | tf_op jit(solution)/shard_map
  198.3 5.2 %gather_fusion = bf16[8,2048,128]{2,1,0:T(8,128)(2,1)} fusion(bf16[8,2048,128]{2,1,0:T(8,128)(2,1)} %copy.30, s32[1024]{0:T(1024)S(1)} %pad_clamp_fusion), kind=kCustom, calls=%fused_computation | custom fusion | bytes 8388640 | tf_op jit(solution)/shard_map/cond/branch_1_fun/jit(_take)/gather | solution.py:76
  203.6 6.5 %copy.22 = bf16[8,2048,128]{1,2,0:T(8,128)(2,1)} copy(bf16[8,2048,128]{2,1,0:T(8,128)(2,1)} %gather_fusion) | data formatting | bytes 8388608 | tf_op jit(solution)/shard_map/cond/branch_1_fun/jit(_take)/gather | solution.py:76
  210.1 2.8 broadcast_select_fusion
  212.9 0.0 copy-done.1
  213.0 0.3 copy-done.4
  213.2 2.4 convert_bitcast_fusion
  215.6 2.1 fusion.1
  217.8 2.1 fusion
  219.8 0.0 copy-done
  219.8 0.0 copy-done.3
  219.8 5.5 %fusion.6 = bf16[4096,512]{0,1:T(8,128)(2,1)} fusion(bf16[128,4096]{1,0:T(8,128)(2,1)S(1)} %copy-done, bf16[2048,128]{0,1:T(8,128)(2,1)} %get-tuple-element.46, f32[512,1024]{1,0:T(8,128)S(1)} %get-tuple-element.44, f32[512,1024]{1,0:T(8,128)} %get-tuple-element.45, bf16[512,3,128]{2,0,1:T(8,128)(2,1)S(1)} %add_convert_fusion, ...), kind=kOutput, calls=%fused_computation.23 | convolution fusion | flops 810942464 | bytes 10224128 | tf_op jit(solution)/shard_map/dot_general | solution.py:104
  225.4 6.5 %copy.33 = bf16[4096,512]{1,0:T(8,128)(2,1)} copy(bf16[4096,512]{0,1:T(8,128)(2,1)} %fusion.6) | data formatting | bytes 8388608
  231.9 0.0 reduce-scatter.4.cloned.1.call-update
  231.9 122.7 %reduce-scatter.4.cloned.1.call-done = bf16[128,512]{1,0:T(8,128)(2,1)} async-done(((bf16[4096,512]{1,0:T(8,128)(2,1)}), bf16[128,512]{1,0:T(8,128)(2,1)}) %reduce-scatter.4.cloned.1.call-update) | async-done | bytes 131088
  354.6 1.7 copy.34
  (8 shorter events, 0.0 us)
Async XLA Ops:
  6.5 213.3 %copy-start = (bf16[128,4096]{1,0:T(8,128)(2,1)S(1)}, bf16[128,4096]{1,0:T(8,128)(2,1)}, u32[]{:S(2)}) copy-start(bf16[128,4096]{1,0:T(8,128)(2,1)} %param.13) | copy-start | bytes 3145732
  6.5 77.8 %all-gather.6.cloned.1.call-start = ((), (), s32[]{:S(2)}) async-start(), calls=%async_computation.1 | async-start | bytes 4325376 | tf_op jit(solution)/shard_map/all_gather | solution.py:42
  7.3 130.6 %all-gather.8.cloned.1.call-start = ((), (), s32[]{:S(2)}) async-start(), calls=%async_computation.2 | async-start | bytes 1179648 | tf_op jit(solution)/shard_map/all_gather | solution.py:61
  8.0 183.8 %all-gather.10.cloned.1.call-start = ((), (), s32[]{:S(2)}) async-start(), calls=%async_computation.3 | async-start | bytes 1179648 | tf_op jit(solution)/shard_map/all_gather | solution.py:88
  84.4 10.5 %copy-start.2 = (bf16[3,3,128]{2,1,0:T(4,128)(2,1)S(1)}, bf16[3,3,128]{2,1,0:T(4,128)(2,1)}, u32[]{:S(2)}) copy-start(bf16[3,3,128]{2,1,0:T(4,128)(2,1)} %param.10) | copy-start | bytes 6916
  89.9 7.9 %collective-permute-start = (bf16[2,3,128]{2,0,1:T(2,128)(2,1)S(1)}, bf16[2,3,128]{2,0,1:T(2,128)(2,1)S(1)}, u32[]{:S(2)}, u32[]{:S(2)}) collective-permute-start(bf16[2,3,128]{2,0,1:T(2,128)(2,1)S(1)} %slice_bitcast_fusion.2), channel_id=1, source_target_pairs={{0,32},{32,64},{64,96},{96,128},{128,160},{160,192},{192,224},{1,3... | collective-permute-start | bytes 4616 | tf_op jit(solution)/shard_map/ppermute | solution.py:13
  98.8 255.8 %reduce-scatter.4.cloned.1.call-start = ((), (), s32[]{:S(2)}) async-start(), calls=%async_computation.4 | async-start | bytes 4325376
  191.8 28.0 %copy-start.3 = (f32[128]{0:T(128)S(1)}, f32[128]{0:T(128)}, u32[]{:S(2)}) copy-start(f32[128]{0:T(128)} %param.11) | copy-start | bytes 1540
  210.1 2.9 copy-start.1
  210.1 3.1 copy-start.4
Sparse Core Ops, SparseCore 0:
  9.1 75.2 all-gather.5
  87.0 50.7 all-gather.7
  140.5 51.2 all-gather.9
  232.0 122.5 reduce-scatter.3
where the time goes:
time: 364 us; the launch traced here: 363 us
  waiting for transfers between devices  234 us (64%)
  other arithmetic  47.2 us (13%)
  local copies, waits for them, and re-layouts  40.2 us (11%)
  matrix products  22.5 us (6%)
  between operations  13.2 us (4%)
  starting transfers between devices  5.22 us (1%)
    unnamed x5, waiting for transfers between devices  124 us
    all_gather x1, waiting for transfers between devices, body(): lax.all_gather(inputs, 'chan', axis=1, tiled=True)  62.3 us
    all_gather x1, waiting for transfers between devices, body(): incoming = lax.all_gather(gated_in[None], 'ctx', axis=0, tiled=True)  36.6 us
    another operation x2, other arithmetic  27.1 us
    unnamed x9, local copies, waits for them, and re-layouts  13 us
    gather x2, local copies, waits for them, and re-layouts, accumulate(): chosen = jnp.take(spectra_taps, jnp.clip(lag_index, 0, groups - 1), axis=0)  11.8 us
    neg x1, other arithmetic, tables(): -jnp.sin(third)  9.1 us
    dot_general x1, matrix products, body(): jnp.einsum('fm,kmd->kfd', forward_taps, padded_taps, preferred_element_ty...  9.05 us
  transfers between devices with their start and end apart: 5, of which 5 were waited for; matrix products, arithmetic and copies ran while one was open for 19% of the time, Pallas kernels for 0%

commit v1 on v0

--- a/solution.py
+++ b/solution.py
@@ -39,7 +39,9 @@
     position = lax.axis_index("ctx")
     w_flat = w_in.reshape(w_in.shape[0], 3 * width_dev)
     projected = jnp.dot(
-        lax.all_gather(inputs, "chan", axis=1, tiled=True),
+        jnp.concatenate(
+            lax.all_to_all(jnp.stack([inputs] * lax.axis_size("chan")), "chan", 0, 0), axis=1
+        ),
         w_flat,
         preferred_element_type=jnp.float32,
     )

time: 364 us -> 351 us (0.964)
  waiting for transfers between devices: 234 us -> 207 us
  starting transfers between devices: 5.22 us -> 15.1 us
  local copies, waits for them, and re-layouts: 40.2 us -> 43.9 us
    all_to_all x0 -> x1, waiting for transfers between devices: none -> 81.9 us  [body(): lax.all_to_all(jnp.stack([inputs] * lax.axis_size('chan')), 'chan', 0, 0)]
    all_gather x1 -> x0, waiting for transfers between devices: 62.3 us -> none  [body(): lax.all_gather(inputs, 'chan', axis=1, tiled=True)]
    all_gather x1, waiting for transfers between devices: 36.6 us -> 0.01 us  [body(): incoming = lax.all_gather(gated_in[None], 'ctx', axis=0, tiled=True)]
    all_to_all x0 -> x1, starting transfers between devices: none -> 10 us  [body(): lax.all_to_all(jnp.stack([inputs] * lax.axis_size('chan')), 'chan', 0, 0)]
    all_gather x1, waiting for transfers between devices: 8.9 us -> 0.01 us  [body(): all_taps = lax.all_gather(filter_taps[None], 'ctx', axis=0, tiled=True)]
    another operation x1 -> x2, local copies, waits for them, and re-layouts: 6.46 us -> 8.9 us
    unnamed x5 -> x4, waiting for transfers between devices: 124 us -> 123 us
    unnamed x9 -> x10, local copies, waits for them, and re-layouts: 13 us -> 14.1 us
  transfers between devices with their start and end apart: 5 -> 5, of which waited for: 5 -> 3; matrix products, arithmetic and copies ran while one was open for 19% -> 20% of each run, Pallas kernels for 0% -> 0%
where the time goes in v1:
time: 351 us; the launch traced here: 350 us
  waiting for transfers between devices  207 us (59%)
  other arithmetic  47.2 us (13%)
  local copies, waits for them, and re-layouts  43.9 us (13%)
  matrix products  22.7 us (6%)
  starting transfers between devices  15.1 us (4%)
  between operations  13.2 us (4%)
    unnamed x4, waiting for transfers between devices  123 us
    all_to_all x1, waiting for transfers between devices, body(): lax.all_to_all(jnp.stack([inputs] * lax.axis_size('chan')), 'chan', 0, 0)  81.9 us
    another operation x2, other arithmetic  27.1 us
    unnamed x10, local copies, waits for them, and re-layouts  14.1 us
    gather x2, local copies, waits for them, and re-layouts, accumulate(): chosen = jnp.take(spectra_taps, jnp.clip(lag_index, 0, groups - 1), axis=0)  11.8 us
    all_to_all x1, starting transfers between devices, body(): lax.all_to_all(jnp.stack([inputs] * lax.axis_size('chan')), 'chan', 0, 0)  10 us
    dot_general x1, matrix products, body(): jnp.einsum('fm,kmd->kfd', forward_taps, padded_taps, preferred_element_ty...  9.15 us
    neg x1, other arithmetic, tables(): -jnp.sin(third)  9.09 us
  transfers between devices with their start and end apart: 5, of which 3 were waited for; matrix products, arithmetic and copies ran while one was open for 20% of the time, Pallas kernels for 0%

profile of v1, /device:TPU:2, one launch (start us, length us, event | category | flops | bytes accessed | tf_op | source)
XLA Modules:
  0.0 349.6 jit_solution(4743522002742137915)
XLA Ops:
  6.5 0.0 copy-start
  6.5 1.1 copy.25
  7.6 2.4 stack.2
  10.1 10.0 %all-to-all-start = ((bf16[32,512,128]{1,2,0:T(8,128)(2,1)}), bf16[32,512,128]{1,2,0:T(8,128)(2,1)}, u32[]{:S(2)}, u32[]{:S(2)}) async-start(bf16[32,512,128]{1,2,0:T(8,128)(2,1)} %stack.2), calls=%async_computation | async-start | bytes 8388608 | tf_op jit(solution)/shard_map/all_to_all | solution.py:43
  20.1 0.0 all-gather.5.cloned.1.call-start
  20.1 0.7 all-gather.5.cloned.1.call-update
  20.8 0.0 all-gather.7.cloned.1.call-start
  20.9 4.7 %copy.26 = bf16[4096,3,128]{0,2,1:T(8,128)(2,1)} copy(bf16[4096,3,128]{2,0,1:T(8,128)(2,1)} %param.9) | data formatting | bytes 6291456 | tf_op args[1]
  25.6 9.3 %negate_convert_fusion.1 = (bf16[1024,512]{1,0:T(8,128)(2,1)}, bf16[1024,512]{1,0:T(8,128)(2,1)}) fusion(), kind=kLoop, calls=%fused_computation.56 | loop fusion | flops 8912896 | bytes 2097152 | tf_op jit(solution)/shard_map/convert.8
  34.9 81.9 %all-to-all-done = bf16[32,512,128]{1,2,0:T(8,128)(2,1)} async-done(((bf16[32,512,128]{1,2,0:T(8,128)(2,1)}), bf16[32,512,128]{1,2,0:T(8,128)(2,1)}, u32[]{:S(2)}, u32[]{:S(2)}) %all-to-all-start) | async-done | bytes 4194336 | tf_op jit(solution)/shard_map/all_to_all | solution.py:43
  116.8 0.0 copy-start.2
  116.8 5.5 %convolution_convert_fusion.1 = bf16[512,384]{1,0:T(8,128)(2,1)S(1)} fusion(bf16[512,4096]{0,1:T(8,128)(2,1)} %bitcast.5, bf16[4096,384]{0,1:T(8,128)(2,1)} %bitcast.57), kind=kOutput, calls=%fused_computation.66 | convolution fusion | flops 1610809344 | bytes 7733248 | tf_op jit(solution)/shard_map/dot_general | solution.py:41
  122.3 4.8 %collective-permute-start = (bf16[2,3,128]{2,0,1:T(2,128)(2,1)S(1)}, bf16[2,3,128]{2,0,1:T(2,128)(2,1)S(1)}, u32[]{:S(2)}, u32[]{:S(2)}) collective-permute-start(bf16[2,3,128]{2,0,1:T(2,128)(2,1)S(1)} %slice_bitcast_fusion.2), channel_id=1, source_target_pairs={{0,32},{32,64},{64,96},{96,128},{128,160},{160,192},{192,224},{1,3... | collective-permute-start | bytes 4616 | tf_op jit(solution)/shard_map/ppermute | solution.py:13
  127.2 0.0 copy-done.2
  127.2 0.2 copy.27
  127.4 0.2 copy.28
  127.6 2.6 collective-permute-done
  130.2 0.3 add_convert_fusion
  130.5 0.7 multiply_convert_fusion
  131.2 0.0 all-gather.7.cloned.1.call-update
  131.2 0.2 reduce-scatter.4.cloned.1.call-start
  131.5 9.1 %sine_negate_fusion = (f32[512,1024]{1,0:T(8,128)S(1)}, f32[512,1024]{1,0:T(8,128)}) fusion(), kind=kLoop, calls=%fused_computation.60 | loop fusion | flops 7864320 | bytes 4194304 | tf_op jit(solution)/shard_map/neg | solution.py:29
  140.6 3.0 pad_maximum_fusion
  143.6 17.8 %negate_convert_fusion = (bf16[1024,1024]{1,0:T(8,128)(2,1)}, bf16[1024,1024]{1,0:T(8,128)(2,1)}) fusion(), kind=kLoop, calls=%fused_computation.34 | loop fusion | flops 17825792 | bytes 4194304 | tf_op jit(solution)/shard_map/convert.6
  161.4 0.0 all-gather.5.cloned.1.call-done
  161.4 2.3 slice.71
  163.7 2.3 copy.31
  166.0 2.3 copy.32
  168.3 1.6 pad_slice_fusion
  169.8 9.1 %convert_bitcast_fusion.1 = bf16[8,2048,128]{1,2,0:T(8,128)(2,1)} fusion(bf16[1024,1024]{1,0:T(8,128)(2,1)} %get-tuple-element.40, bf16[1024,1024]{1,0:T(8,128)(2,1)} %get-tuple-element.41, bf16[8,511,128]{1,2,0:T(8,128)(2,1)S(1)} %pad_slice_fusion, bf16[8,512,128]{1,2,0:T(8,128)(2,1)} %copy.32, bf16[1024]{0:T(1024)(128)(2,1)S(1)} %pad.8.clone), kind=kOutput, calls=%fused_computation.33 | convolution fusion | flops 4311744512 | bytes 10485760 | tf_op jit(solution)/shard_map/fm,kmd->kfd/dot_general | solution.py:70
  179.0 0.0 all-gather.7.cloned.1.call-done
  179.0 28.1 %conditional.1 = (bf16[2048,128]{0,1:T(8,128)(2,1)}) conditional(s32[]{:T(128)} %convert_element_type.147, () %tuple.13, (s32[]{:T(128)}, bf16[8,2048,128]{1,2,0:T(8,128)(2,1)}, bf16[8,512,128]{2,1,0:T(8,128)(2,1)}, bf16[2048,512]{1,0:T(8,128)(2,1)}) %tuple.33), branch_computations={%region_0.1_spmd, %region_1.3_spmd} | conditional | flops 2168194048 | bytes 79171784 | solution.py:101
  179.0 6.5 %copy.33 = bf16[8,2048,128]{2,1,0:T(8,128)(2,1)} copy(bf16[8,2048,128]{1,2,0:T(8,128)(2,1)} %get-tuple-element.30) | data formatting | bytes 8388608 | tf_op jit(solution)/shard_map
  185.5 5.4 %gather_fusion = bf16[8,2048,128]{2,1,0:T(8,128)(2,1)} fusion(bf16[8,2048,128]{2,1,0:T(8,128)(2,1)} %copy.33, s32[1024]{0:T(1024)S(1)} %pad_clamp_fusion), kind=kCustom, calls=%fused_computation | custom fusion | bytes 8388640 | tf_op jit(solution)/shard_map/cond/branch_1_fun/jit(_take)/gather | solution.py:78
  190.9 6.5 %copy.24 = bf16[8,2048,128]{1,2,0:T(8,128)(2,1)} copy(bf16[8,2048,128]{2,1,0:T(8,128)(2,1)} %gather_fusion) | data formatting | bytes 8388608 | tf_op jit(solution)/shard_map/cond/branch_1_fun/jit(_take)/gather | solution.py:78
  197.3 2.8 broadcast_select_fusion
  200.1 0.0 copy-done.1
  200.2 0.3 copy-done.4
  200.5 2.4 convert_bitcast_fusion
  202.8 2.1 fusion.1
  205.0 2.1 fusion
  207.1 0.0 copy-done
  207.1 0.0 copy-done.3
  207.1 5.6 %fusion.6 = bf16[4096,512]{0,1:T(8,128)(2,1)} fusion(bf16[128,4096]{1,0:T(8,128)(2,1)S(1)} %copy-done, bf16[2048,128]{0,1:T(8,128)(2,1)} %get-tuple-element.46, f32[512,1024]{1,0:T(8,128)S(1)} %get-tuple-element.44, f32[512,1024]{1,0:T(8,128)} %get-tuple-element.45, bf16[512,3,128]{2,0,1:T(8,128)(2,1)S(1)} %add_convert_fusion, ...), kind=kOutput, calls=%fused_computation.23 | convolution fusion | flops 810942464 | bytes 10224128 | tf_op jit(solution)/shard_map/dot_general | solution.py:106
  212.7 6.6 %copy.36 = bf16[4096,512]{1,0:T(8,128)(2,1)} copy(bf16[4096,512]{0,1:T(8,128)(2,1)} %fusion.6) | data formatting | bytes 8388608
  219.3 0.0 reduce-scatter.4.cloned.1.call-update
  219.3 122.1 %reduce-scatter.4.cloned.1.call-done = bf16[128,512]{1,0:T(8,128)(2,1)} async-done(((bf16[4096,512]{1,0:T(8,128)(2,1)}), bf16[128,512]{1,0:T(8,128)(2,1)}) %reduce-scatter.4.cloned.1.call-update) | async-done | bytes 131088
  341.4 1.7 copy.37
  (9 shorter events, 0.1 us)
Async XLA Ops:
  6.5 200.5 %copy-start = (bf16[128,4096]{1,0:T(8,128)(2,1)S(1)}, bf16[128,4096]{1,0:T(8,128)(2,1)}, u32[]{:S(2)}) copy-start(bf16[128,4096]{1,0:T(8,128)(2,1)} %param.13) | copy-start | bytes 3145732
  10.1 106.7 %all-to-all-start = ((bf16[32,512,128]{1,2,0:T(8,128)(2,1)}), bf16[32,512,128]{1,2,0:T(8,128)(2,1)}, u32[]{:S(2)}, u32[]{:S(2)}) async-start(bf16[32,512,128]{1,2,0:T(8,128)(2,1)} %stack.2), calls=%async_computation | async-start | bytes 8388608 | tf_op jit(solution)/shard_map/all_to_all | solution.py:43
  20.1 141.3 %all-gather.5.cloned.1.call-start = ((), (), s32[]{:S(2)}) async-start(), calls=%async_computation.2 | async-start | bytes 1179648 | tf_op jit(solution)/shard_map/all_gather | solution.py:63
  20.8 158.2 %all-gather.7.cloned.1.call-start = ((), (), s32[]{:S(2)}) async-start(), calls=%async_computation.3 | async-start | bytes 1179648 | tf_op jit(solution)/shard_map/all_gather | solution.py:90
  116.8 10.4 %copy-start.2 = (bf16[3,3,128]{2,1,0:T(4,128)(2,1)S(1)}, bf16[3,3,128]{2,1,0:T(4,128)(2,1)}, u32[]{:S(2)}) copy-start(bf16[3,3,128]{2,1,0:T(4,128)(2,1)} %param.10) | copy-start | bytes 6916
  122.3 7.9 %collective-permute-start = (bf16[2,3,128]{2,0,1:T(2,128)(2,1)S(1)}, bf16[2,3,128]{2,0,1:T(2,128)(2,1)S(1)}, u32[]{:S(2)}, u32[]{:S(2)}) collective-permute-start(bf16[2,3,128]{2,0,1:T(2,128)(2,1)S(1)} %slice_bitcast_fusion.2), channel_id=1, source_target_pairs={{0,32},{32,64},{64,96},{96,128},{128,160},{160,192},{192,224},{1,3... | collective-permute-start | bytes 4616 | tf_op jit(solution)/shard_map/ppermute | solution.py:13
  131.2 210.1 %reduce-scatter.4.cloned.1.call-start = ((), (), s32[]{:S(2)}) async-start(), calls=%async_computation.4 | async-start | bytes 4325376
  179.0 28.1 %copy-start.3 = (f32[128]{0:T(128)S(1)}, f32[128]{0:T(128)}, u32[]{:S(2)}) copy-start(f32[128]{0:T(128)} %param.11) | copy-start | bytes 1540
  197.3 2.9 copy-start.1
  197.3 3.1 copy-start.4
Sparse Core Ops, SparseCore 0:
  23.6 56.7 all-gather.4
  131.3 47.5 all-gather.6
  219.4 121.9 reduce-scatter.3
